TPU v7x, 32 devices: a whole 2x2x4 slice. The times are simulated.
32 devices in a mesh: edata: 4 (over z), expert: 8 (over y, x, core).
Axes of the slice: x: 2, y: 2, z: 4, core: 2. Of those that a mesh axis runs over, the one named last changes fastest.
Arguments:
- tokens: bfloat16 [1024, 4096], P('expert', 'edata'), may hold values from -6 to 6
- grad_out: bfloat16 [1024, 4096], P('expert', 'edata'), may hold values from -6 to 6
- expert_ids: int32 [1024, 8], P('expert'), may hold values from 0 to 15, all different within a row; in each aligned block of 128 rows (0 to 127, 128 to 255, ...) at most 80 rows name the same one
- route_prob: float32 [1024, 8], P('expert'), may hold values from 0.05 to 0.5
- w_gate: bfloat16 [16, 1024, 4096], P('expert', 'edata'), may hold values from -0.09375 to 0.09375
- w_up: bfloat16 [16, 1024, 4096], P('expert', 'edata'), may hold values from -0.09375 to 0.09375
- w_down: bfloat16 [16, 1024, 4096], P('expert', 'edata'), may hold values from -0.1875 to 0.1875
Outputs:
- grad_tokens: bfloat16 [1024, 4096], P('expert', 'edata')
- grad_gate: bfloat16 [16, 1024, 4096], P('expert', 'edata')
- grad_up: bfloat16 [16, 1024, 4096], P('expert', 'edata')
- grad_down: bfloat16 [16, 1024, 4096], P('expert', 'edata')
Inputs may be any that keep to these rules, and one draw needn't show every extreme that they name: `expert_ids`: each token names 8 different experts. Among the tokens of one aligned block of 128 no expert is named more than 80 times, and in every draw some expert is named exactly 80 times in some block.
All inputs are finite; a program needn't handle non-finite values.
Results may differ from a plain program's by a relative error of at most 0.012.
Values may be sent and summed in bfloat16 or wider, within the bound.
A program may use at most 192 MiB of HBM per device.

v0:
```python
import jax
import jax.numpy as jnp
from jax import lax
from jax.sharding import PartitionSpec as P


def ranks(onehot):
    pair_count = onehot.shape[-2]
    row = lax.broadcasted_iota(jnp.int32, (pair_count, pair_count), 0)
    col = lax.broadcasted_iota(jnp.int32, (pair_count, pair_count), 1)
    tri = (col < row).astype(jnp.bfloat16)
    earlier = jnp.einsum(
        "pq,...qe->...pe", tri, onehot.astype(jnp.bfloat16), preferred_element_type=jnp.float32
    )
    return earlier.astype(jnp.int32)


def body(tokens, grad_out, expert_ids, route_prob, w_gate, w_up, w_down):
    token_count, top_count = expert_ids.shape
    local_experts = w_gate.shape[0]
    expert_devices = lax.axis_size("expert")
    me = lax.axis_index("expert")
    experts_all = expert_devices * local_experts
    capacity = token_count * top_count * 5 // (4 * experts_all)
    pair_count = token_count * top_count
    cap_iota = jnp.arange(capacity, dtype=jnp.int32)
    routing = jnp.stack([expert_ids.astype(jnp.float32), route_prob])
    routing = lax.all_gather(routing, "expert", axis=1, tiled=False)
    all_ids, all_prob = (routing[0].astype(jnp.int32), routing[1])
    mine = me * local_experts + jnp.arange(local_experts, dtype=jnp.int32)
    named = all_ids.reshape(expert_devices, pair_count)[:, :, None] == mine
    rank = ranks(named)
    hit = named[..., None] & (rank[..., None] == cap_iota)
    hit = hit.reshape(expert_devices, token_count, top_count, local_experts, capacity)
    pick = jnp.sum(hit.astype(jnp.int32), 2).astype(jnp.bfloat16)
    prob_of = jnp.sum(jnp.where(hit, all_prob[:, :, :, None, None], 0.0), (1, 2))
    both = lax.all_gather(jnp.stack([tokens, grad_out]), "edata", axis=2, tiled=True)
    both = lax.all_gather(both, "expert", axis=1, tiled=False)
    all_x, all_dy = (both[0], both[1])
    slot_x = jnp.einsum("stxc,std->sxcd", pick, all_x, preferred_element_type=jnp.float32).astype(
        jnp.bfloat16
    )
    slot_dy = jnp.einsum("stxc,std->sxcd", pick, all_dy, preferred_element_type=jnp.float32)
    slot_dy = (prob_of[..., None] * slot_dy).astype(jnp.bfloat16)
    gate_value = jnp.einsum("sxcd,xfd->sxcf", slot_x, w_gate, preferred_element_type=jnp.float32)
    up_value = jnp.einsum("sxcd,xfd->sxcf", slot_x, w_up, preferred_element_type=jnp.float32)
    sigma = jax.nn.sigmoid(gate_value)
    active = gate_value * sigma
    hidden = (active * up_value).astype(jnp.bfloat16)
    back = jnp.einsum("sxcd,xfd->sxcf", slot_dy, w_down, preferred_element_type=jnp.float32)
    gate_grad = (back * up_value * sigma * (1.0 + gate_value * (1.0 - sigma))).astype(jnp.bfloat16)
    up_grad = (back * active).astype(jnp.bfloat16)
    grad_gate = jnp.einsum(
        "sxcf,sxcd->xfd", gate_grad, slot_x, preferred_element_type=jnp.float32
    ).astype(jnp.bfloat16)
    grad_up = jnp.einsum(
        "sxcf,sxcd->xfd", up_grad, slot_x, preferred_element_type=jnp.float32
    ).astype(jnp.bfloat16)
    grad_down = jnp.einsum(
        "sxcf,sxcd->xfd", hidden, slot_dy, preferred_element_type=jnp.float32
    ).astype(jnp.bfloat16)
    partial_value = jnp.einsum(
        "sxcf,xfd->sxcd", gate_grad, w_gate, preferred_element_type=jnp.float32
    )
    partial_value = partial_value + jnp.einsum(
        "sxcf,xfd->sxcd", up_grad, w_up, preferred_element_type=jnp.float32
    )
    partial_value = partial_value.astype(jnp.bfloat16)
    returned = lax.all_to_all(
        partial_value.reshape(expert_devices, local_experts * capacity, -1),
        "expert",
        split_axis=0,
        concat_axis=0,
        tiled=True,
    )
    width = returned.shape[-1]
    own = expert_ids.reshape(pair_count, 1) == jnp.arange(experts_all, dtype=jnp.int32)
    slot = jnp.sum(jnp.where(own, ranks(own), 0), 1)
    back_hit = own[:, :, None] & (slot[:, None, None] == cap_iota)
    gather_back = jnp.sum(
        back_hit.reshape(token_count, top_count, experts_all * capacity).astype(jnp.int32), 1
    ).astype(jnp.bfloat16)
    per_token = jnp.einsum(
        "tq,qd->td",
        gather_back,
        returned.reshape(experts_all * capacity, width),
        preferred_element_type=jnp.float32,
    )
    grad_tokens = lax.psum_scatter(per_token, "edata", scatter_dimension=1, tiled=True).astype(
        jnp.bfloat16
    )
    return (grad_tokens, grad_gate, grad_up, grad_down)


def solution(mesh):
    placed = (
        P("expert", "edata"),
        P("expert", "edata"),
        P("expert", None),
        P("expert", None),
        P("expert", "edata", None),
        P("expert", "edata", None),
        P("expert", "edata", None),
    )
    return jax.shard_map(
        body,
        mesh=mesh,
        in_specs=placed,
        out_specs=(
            P("expert", "edata"),
            P("expert", "edata", None),
            P("expert", "edata", None),
            P("expert", "edata", None),
        ),
        check_vma=False,
    )
```

profile of v0, /device:TPU:0, one launch (start us, length us, event | category | flops | bytes accessed | tf_op | source)
XLA Modules:
  0.0 408.3 jit_solution(9152429621475397026)
XLA Ops:
  7.2 1.9 pad_maximum_fusion
  9.2 49.4 %all-gather.5.cloned.1.call-done = bf16[2,128,4096]{2,1,0:T(8,128)(2,1)} async-done(((bf16[2,128,1024]{2,1,0:T(8,128)(2,1)}), bf16[2,128,4096]{2,1,0:T(8,128)(2,1)}) %all-gather.5.cloned.1.call-update) | async-done | bytes 2097168 | tf_op jit(solution)/shard_map/all_gather | solution.py:37
  59.9 9.0 %all-gather = f32[2,1024,8]{1,2,0:T(8,128)S(1)} all-gather(f32[2,128,8]{1,2,0:T(8,128)S(1)} %pad_maximum_fusion.1), channel_id=2, replica_groups=mesh['edata'=4,'expert'=8] {'expert'}, dimensions={1}, use_global_device_ids=true | all-gather | bytes 73728 | tf_op jit(solution)/shard_map/all_gather | solution.py:28
  73.7 75.3 %all-gather.7.cloned.1.call-done = bf16[2,1024,4096]{2,1,0:T(8,128)(2,1)} async-done(((bf16[2,128,4096]{2,1,0:T(8,128)(2,1)}), bf16[2,1024,4096]{2,1,0:T(8,128)(2,1)}) %all-gather.7.cloned.1.call-update) | async-done | bytes 16777232 | tf_op jit(solution)/shard_map/all_gather | solution.py:38
  149.0 9.5 %fusion.65 = (bf16[1,1024,4096]{2,1,0:T(8,128)(2,1)}, bf16[1,1024,4096]{2,1,0:T(8,128)(2,1)S(1)}) fusion(bf16[2,1024,4096]{2,1,0:T(8,128)(2,1)} %all-gather.7.cloned.1.call-done), kind=kLoop, calls=%fused_computation.65 | loop fusion | bytes 33554432 | tf_op jit(solution)/shard_map/slice | solution.py:39
  158.5 5.5 %convolution_convert_fusion = bf16[8,2,80,4096]{3,2,1,0:T(8,128)(2,1)} fusion(bf16[8,128,4096,1]{2,1,3,0:T(8,128)(2,1)S(1)} %bitcast.84, s32[8,128,2,80]{1,3,2,0:T(8,128)S(1)} %convert_reduce_fusion), kind=kOutput, calls=%fused_computation.11 | convolution fusion | flops 1347584000 | bytes 19529728 | tf_op jit(solution)/shard_map/stxc,std->sxcd/dot_general | solution.py:40
  163.9 9.3 %fusion.35 = f32[8,2,80,256]{3,2,0,1:T(8,128)} fusion(bf16[2,256,4096]{2,1,0:T(8,128)(2,1)} %param.11, bf16[8,2,80,4096]{3,2,1,0:T(8,128)(2,1)} %convolution_convert_fusion), kind=kOutput, calls=%fused_computation.35 | convolution fusion | flops 2684354560 | bytes 15990784 | tf_op jit(solution)/shard_map/sxcd,xfd->sxcf/dot_general | solution.py:45
  173.2 9.3 %fusion.30 = f32[8,2,80,256]{3,2,0,1:T(8,128)} fusion(bf16[2,256,4096]{2,1,0:T(8,128)(2,1)} %param.12, bf16[8,2,80,4096]{3,2,1,0:T(8,128)(2,1)} %convolution_convert_fusion), kind=kOutput, calls=%fused_computation.34 | convolution fusion | flops 2684354560 | bytes 15990784 | tf_op jit(solution)/shard_map/sxcd,xfd->sxcf/dot_general | solution.py:46
  182.5 5.4 %multiply_convert_fusion = bf16[8,2,80,4096]{3,2,1,0:T(8,128)(2,1)} fusion(f32[8,2,80]{2,1,0:T(2,128)S(1)} %select_reduce_fusion, bf16[8,128,4096,1]{2,1,3,0:T(8,128)(2,1)S(1)} %bitcast.87, s32[8,128,2,80]{1,3,2,0:T(8,128)S(1)} %convert_reduce_fusion), kind=kOutput, calls=%fused_computation.1 | convolution fusion | flops 1352826880 | bytes 19534848 | tf_op jit(solution)/shard_map/stxc,std->sxcd/dot_general | solution.py:43
  187.9 9.4 %multiply_convert_fusion.2 = (bf16[8,2,80,256]{3,2,0,1:T(8,128)(2,1)S(1)}, bf16[8,2,80,256]{3,2,0,1:T(8,128)(2,1)S(1)}) fusion(f32[8,2,80,256]{3,2,0,1:T(8,128)} %fusion.35, f32[8,2,80,256]{3,2,0,1:T(8,128)} %fusion.30, bf16[2,256,4096]{2,1,0:T(8,128)(2,1)} %param.13, bf16[8,2,80,4096]{3,2,1,0:T(8,128)(2,1)} %multiply_convert_fusion), kind=kOutput, calls=%fused_computation.38 | convolution fusion | flops 2688614400 | bytes 18612224 | tf_op jit(solution)/shard_map/sxcd,xfd->sxcf/dot_general | solution.py:50
  197.3 8.7 %fusion.20 = f32[2,8,80,4096]{3,2,1,0:T(8,128)} fusion(bf16[8,2,80,256]{3,2,0,1:T(8,128)(2,1)S(1)} %get-tuple-element.7, bf16[2,256,4096]{2,1,0:T(8,128)(2,1)S(1)} %copy-done), kind=kOutput, calls=%fused_computation.24 | convolution fusion | flops 2684354560 | bytes 25821184 | tf_op jit(solution)/shard_map/sxcf,xfd->sxcd/dot_general | solution.py:62
  206.0 13.0 %fusion = bf16[8,2,80,4096]{3,2,0,1:T(8,128)(2,1)} fusion(f32[2,8,80,4096]{3,2,1,0:T(8,128)} %fusion.20, bf16[8,2,80,256]{3,2,0,1:T(8,128)(2,1)S(1)} %get-tuple-element.6, bf16[2,256,4096]{2,1,0:T(8,128)(2,1)} %param.12), kind=kOutput, calls=%fused_computation.2 | convolution fusion | flops 2694840320 | bytes 36306944 | tf_op jit(solution)/shard_map/sxcf,xfd->sxcd/dot_general | solution.py:65
  219.0 9.4 %copy.42 = bf16[8,2,80,4096]{3,2,1,0:T(8,128)(2,1)} copy(bf16[8,2,80,4096]{3,2,0,1:T(8,128)(2,1)} %fusion) | data formatting | bytes 20971520 | tf_op jit(solution)/shard_map/convert_element_type | solution.py:68
  228.4 5.3 %all-to-all-start = ((bf16[8,160,4096]{2,1,0:T(8,128)(2,1)}), bf16[8,160,4096]{2,1,0:T(8,128)(2,1)}, u32[]{:S(2)}, u32[]{:S(2)}) async-start(bf16[8,160,4096]{2,1,0:T(8,128)(2,1)} %bitcast.83), calls=%async_computation | async-start | bytes 20971520 | tf_op jit(solution)/shard_map/all_to_all | solution.py:69
  235.0 7.9 %and_convert_fusion = s32[1024,16,80]{2,1,0:T(8,128)} fusion(pred[1024,80]{1,0:T(8,128)(4,1)S(1)} %iota_compare_fusion.9, pred[1024,16]{1,0:T(8,128)(4,1)S(1)} %copy.35), kind=kLoop, calls=%fused_computation.10 | loop fusion | flops 2621440 | bytes 5341184 | tf_op jit(solution)/shard_map/convert_element_type | solution.py:81
  242.8 9.1 %reshape.90 = s32[128,8,1280]{2,1,0:T(8,128)} reshape(s32[1024,16,80]{2,1,0:T(8,128)} %and_convert_fusion) | data formatting | bytes 10485760 | tf_op jit(solution)/shard_map/convert_element_type | solution.py:81
  251.9 3.7 reduce_sum.37
  255.7 94.6 %all-to-all-done = bf16[8,160,4096]{2,1,0:T(8,128)(2,1)} async-done(((bf16[8,160,4096]{2,1,0:T(8,128)(2,1)}), bf16[8,160,4096]{2,1,0:T(8,128)(2,1)}, u32[]{:S(2)}, u32[]{:S(2)}) %all-to-all-start) | async-done | bytes 10485792 | tf_op jit(solution)/shard_map/all_to_all | solution.py:69
  350.2 6.8 %fusion.55 = f32[128,4096]{1,0:T(8,128)} fusion(bf16[1280,4096]{1,0:T(8,128)(2,1)} %bitcast.26, s32[128,1280]{1,0:T(8,128)S(1)} %reduce_sum.37), kind=kOutput, calls=%fused_computation.49 | convolution fusion | flops 1342341120 | bytes 13238272 | tf_op jit(solution)/shard_map/tq,qd->td/dot_general | solution.py:83
  357.1 9.2 %bitcast_convert_fusion.1 = bf16[2,256,4096]{2,1,0:T(8,128)(2,1)} fusion(bf16[8,2,80,256]{3,2,0,1:T(8,128)(2,1)S(1)} %get-tuple-element.6, bf16[8,2,80,4096]{3,2,1,0:T(8,128)(2,1)} %convolution_convert_fusion), kind=kOutput, calls=%fused_computation.8 | convolution fusion | flops 2686451712 | bytes 15335424 | tf_op jit(solution)/shard_map/sxcf,sxcd->xfd/dot_general | solution.py:56
  366.3 9.3 %bitcast_convert_fusion.2 = bf16[2,256,4096]{2,1,0:T(8,128)(2,1)} fusion(bf16[8,2,80,256]{3,2,0,1:T(8,128)(2,1)S(1)} %get-tuple-element.7, bf16[8,2,80,4096]{3,2,1,0:T(8,128)(2,1)} %convolution_convert_fusion), kind=kOutput, calls=%fused_computation.9 | convolution fusion | flops 2686451712 | bytes 15335424 | tf_op jit(solution)/shard_map/sxcf,sxcd->xfd/dot_general | solution.py:53
  375.6 5.3 %bitcast_convert_fusion = bf16[2,256,4096]{2,1,0:T(8,128)(2,1)} fusion(bf16[8,2,80,4096]{3,2,1,0:T(8,128)(2,1)S(1)} %bitcast.89, f32[8,2,80,256]{3,2,0,1:T(8,128)S(1)} %copy-done.3, f32[8,2,80,256]{3,2,0,1:T(8,128)S(1)} %copy-done.2), kind=kOutput, calls=%fused_computation.7 | convolution fusion | flops 2688417792 | bytes 17301504 | tf_op jit(solution)/shard_map/sxcf,sxcd->xfd/dot_general | solution.py:59
  381.0 19.0 %reduce-scatter.2.cloned.1.call-done = f32[128,1024]{1,0:T(8,128)} async-done(((f32[128,4096]{1,0:T(8,128)}), f32[128,1024]{1,0:T(8,128)}) %reduce-scatter.2.cloned.1.call-update) | async-done | bytes 524304 | tf_op jit(solution)/shard_map/reduce_scatter | solution.py:89
  400.0 1.8 convert_element_type.96
  (45 shorter events, 7.4 us)
Async XLA Ops:
  7.2 51.4 %all-gather.5.cloned.1.call-start = ((), (), s32[]{:S(2)}) async-start(), calls=%async_computation.2 | async-start | bytes 2621440 | tf_op jit(solution)/shard_map/all_gather | solution.py:37
  9.1 139.9 %all-gather.7.cloned.1.call-start = ((), (), s32[]{:S(2)}) async-start(), calls=%async_computation.4 | async-start | bytes 18874368 | tf_op jit(solution)/shard_map/all_gather | solution.py:38
  163.9 18.6 %slice-start = ((s8[8388608]{0:T(1024)(128)(4,1)}), s8[4194304]{0:T(1024)(128)(4,1)S(1)}, s32[]{:S(2)}) async-start(s8[8388608]{0:T(1024)(128)(4,1)} %bitcast.85), calls=%async_computation.5 | async-start | bytes 8388608
  173.2 9.3 %slice-start.1 = ((s8[8388608]{0:T(1024)(128)(4,1)}), s8[4194304]{0:T(1024)(128)(4,1)S(1)}, s32[]{:S(2)}) async-start(s8[8388608]{0:T(1024)(128)(4,1)} %bitcast.85), calls=%async_computation.6 | async-start | bytes 8388608
  187.9 9.4 %copy-start = (bf16[2,256,4096]{2,1,0:T(8,128)(2,1)S(1)}, bf16[2,256,4096]{2,1,0:T(8,128)(2,1)}, u32[]{:S(2)}) copy-start(bf16[2,256,4096]{2,1,0:T(8,128)(2,1)} %param.11) | copy-start | bytes 12582916
  228.4 5.4 %copy-start.1 = (s32[128,8]{0,1:T(8,128)S(1)}, s32[128,8]{0,1:T(8,128)}, u32[]{:S(2)}) copy-start(s32[128,8]{0,1:T(8,128)} %param.9) | copy-start | bytes 12292
  228.4 121.8 %all-to-all-start = ((bf16[8,160,4096]{2,1,0:T(8,128)(2,1)}), bf16[8,160,4096]{2,1,0:T(8,128)(2,1)}, u32[]{:S(2)}, u32[]{:S(2)}) async-start(bf16[8,160,4096]{2,1,0:T(8,128)(2,1)} %bitcast.83), calls=%async_computation | async-start | bytes 20971520 | tf_op jit(solution)/shard_map/all_to_all | solution.py:69
  233.7 166.3 %reduce-scatter.2.cloned.1.call-start = ((), (), s32[]{:S(2)}) async-start(), calls=%async_computation.3 | async-start | bytes 2621440 | tf_op jit(solution)/shard_map/reduce_scatter | solution.py:89
  357.1 18.5 %slice-start.2 = ((s8[10485760]{0:T(1024)(128)(4,1)}), s8[4194304]{0:T(1024)(128)(4,1)S(1)}, s32[]{:S(2)}) async-start(s8[10485760]{0:T(1024)(128)(4,1)} %bitcast.88), calls=%async_computation.7 | async-start | bytes 8388608
  357.1 18.5 %slice-start.3 = ((s8[10485760]{0:T(1024)(128)(4,1)}), s8[4194304]{0:T(1024)(128)(4,1)S(1)}, s32[]{:S(2)}) async-start(s8[10485760]{0:T(1024)(128)(4,1)} %bitcast.88), calls=%async_computation.8 | async-start | bytes 8388608
  366.3 9.3 %slice-start.4 = ((s8[10485760]{0:T(1024)(128)(4,1)}), s8[2097152]{0:T(1024)(128)(4,1)S(1)}, s32[]{:S(2)}) async-start(s8[10485760]{0:T(1024)(128)(4,1)} %bitcast.88), calls=%async_computation.9 | async-start | bytes 4194304
  366.3 9.3 %copy-start.2 = (f32[8,2,80,256]{3,2,0,1:T(8,128)S(1)}, f32[8,2,80,256]{3,2,0,1:T(8,128)}, u32[]{:S(2)}) copy-start(f32[8,2,80,256]{3,2,0,1:T(8,128)} %fusion.35) | copy-start | bytes 3932164
  366.3 9.3 %copy-start.3 = (f32[8,2,80,256]{3,2,0,1:T(8,128)S(1)}, f32[8,2,80,256]{3,2,0,1:T(8,128)}, u32[]{:S(2)}) copy-start(f32[8,2,80,256]{3,2,0,1:T(8,128)} %fusion.30) | copy-start | bytes 3932164
Sparse Core Ops, SparseCore 0:
  10.1 48.3 all-gather.4
  60.4 88.5 all-gather.6
  357.2 42.7 reduce-scatter.1
where the time goes:
time: 409 us; the launch traced here: 408 us
  waiting for transfers between devices  238 us (58%)
  matrix products  92.1 us (23%)
  local copies, waits for them, and re-layouts  29.9 us (7%)
  other arithmetic  19.5 us (5%)
  between operations  13.9 us (3%)
  blocking collectives  9.03 us (2%)
  starting transfers between devices  5.41 us (1%)
    all_to_all x1, waiting for transfers between devices, body(): lax.all_to_all(partial_value.reshape(expert_devices, local_experts * capa...  94.6 us
    all_gather x1, waiting for transfers between devices, body(): both = lax.all_gather(both, 'expert', axis=1, tiled=False)  75.3 us
    all_gather x1, waiting for transfers between devices, body(): lax.all_gather(jnp.stack([tokens, grad_out]), 'edata', axis=2, tiled=True)  49.4 us
    reduce_scatter x1, waiting for transfers between devices, body(): lax.psum_scatter(per_token, 'edata', scatter_dimension=1, tiled=True)  19 us
    dot_general x1, matrix products, body(): jnp.einsum('sxcf,xfd->sxcd', up_grad, w_up, preferred_element_type=jnp.fl...  13 us
    slice x1, local copies, waits for them, and re-layouts, body(): all_x, all_dy = (both[0], both[1])  9.49 us
    convert_element_type x1, local copies, waits for them, and re-layouts, body(): partial_value = partial_value.astype(jnp.bfloat16)  9.44 us
    dot_general x1, matrix products, body(): jnp.einsum('sxcd,xfd->sxcf', slot_dy, w_down, preferred_element_type=jnp....  9.36 us
  transfers between devices with their start and end apart: 4, of which 4 were waited for; matrix products, arithmetic and copies ran while one was open for 13% of the time, Pallas kernels for 0%

commit v1 on v0

--- a/solution.py
+++ b/solution.py
@@ -34,7 +34,16 @@
     hit = hit.reshape(expert_devices, token_count, top_count, local_experts, capacity)
     pick = jnp.sum(hit.astype(jnp.int32), 2).astype(jnp.bfloat16)
     prob_of = jnp.sum(jnp.where(hit, all_prob[:, :, :, None, None], 0.0), (1, 2))
-    both = lax.all_gather(jnp.stack([tokens, grad_out]), "edata", axis=2, tiled=True)
+    x = jnp.stack([tokens, grad_out])
+    ways, here = (lax.axis_size("edata"), lax.axis_index("edata"))
+    grown, reach = (x, 1)
+    while reach < ways:
+        theirs = lax.ppermute(grown, "edata", [(d, d ^ reach) for d in range(ways)])
+        mine_first = jnp.concatenate([grown, theirs], axis=2)
+        theirs_first = jnp.concatenate([theirs, grown], axis=2)
+        grown = jnp.where(here & reach == 0, mine_first, theirs_first)
+        reach = 2 * reach
+    both = grown
     both = lax.all_gather(both, "expert", axis=1, tiled=False)
     all_x, all_dy = (both[0], both[1])
     slot_x = jnp.einsum("stxc,std->sxcd", pick, all_x, preferred_element_type=jnp.float32).astype(

time: 409 us -> 421 us (1.029)
  local copies, waits for them, and re-layouts: 29.9 us -> 20.4 us
  waiting for transfers between devices: 238 us -> 246 us
  starting transfers between devices: 5.41 us -> 11.4 us
  matrix products: 92.1 us -> 97.1 us
    ppermute x0 -> x2, waiting for transfers between devices: none -> 55.3 us  [body(): theirs = lax.ppermute(grown, 'edata', [(d, d ^ reach) for d in range(ways)])]
    all_gather x1 -> x0, waiting for transfers between devices: 49.4 us -> none  [body(): lax.all_gather(jnp.stack([tokens, grad_out]), 'edata', axis=2, tiled=True)]
    slice x1 -> x0, local copies, waits for them, and re-layouts: 9.49 us -> none  [body(): all_x, all_dy = (both[0], both[1])]
    ppermute x0 -> x2, starting transfers between devices: none -> 5.94 us  [body(): theirs = lax.ppermute(grown, 'edata', [(d, d ^ reach) for d in range(ways)])]
    dot_general x1, matrix products: 5.46 us -> 10.2 us  [body(): jnp.einsum('stxc,std->sxcd', pick, all_x, preferred_element_type=jnp.floa...]
  transfers between devices with their start and end apart: 4 -> 5, of which waited for: 4 -> 5; matrix products, arithmetic and copies ran while one was open for 13% -> 12% of each run, Pallas kernels for 0% -> 0%
where the time goes in v1:
time: 421 us
  waiting for transfers between devices  246 us (58%)
  matrix products  97.1 us (23%)
  other arithmetic  22.7 us (5%)
  local copies, waits for them, and re-layouts  20.4 us (5%)
  between operations  14.2 us (3%)
  starting transfers between devices  11.4 us (3%)
  blocking collectives  8.98 us (2%)
    all_to_all x1, waiting for transfers between devices, body(): lax.all_to_all(partial_value.reshape(expert_devices, local_experts * capa...  94.4 us
    all_gather x1, waiting for transfers between devices, body(): both = lax.all_gather(both, 'expert', axis=1, tiled=False)  77.2 us
    ppermute x2, waiting for transfers between devices, body(): theirs = lax.ppermute(grown, 'edata', [(d, d ^ reach) for d in range(ways)])  55.3 us
    reduce_scatter x1, waiting for transfers between devices, body(): lax.psum_scatter(per_token, 'edata', scatter_dimension=1, tiled=True)  19 us
    dot_general x1, matrix products, body(): jnp.einsum('sxcf,xfd->sxcd', up_grad, w_up, preferred_element_type=jnp.fl...  13 us
    dot_general x1, matrix products, body(): jnp.einsum('stxc,std->sxcd', pick, all_x, preferred_element_type=jnp.floa...  10.2 us
    convert_element_type x1, local copies, waits for them, and re-layouts, body(): partial_value = partial_value.astype(jnp.bfloat16)  9.45 us
    dot_general x1, matrix products, body(): jnp.einsum('sxcd,xfd->sxcf', slot_dy, w_down, preferred_element_type=jnp....  9.36 us
  transfers between devices with their start and end apart: 5, of which 5 were waited for; matrix products, arithmetic and copies ran while one was open for 12% of the time, Pallas kernels for 0%

profile of v1, /device:TPU:0, one launch (start us, length us, event | category | flops | bytes accessed | tf_op | source)
XLA Modules:
  0.0 420.7 jit_solution(1484195299818669656)
XLA Ops:
  8.3 3.1 collective-permute-start
  11.4 11.9 %collective-permute-done = bf16[2,128,1024]{2,1,0:T(8,128)(2,1)S(1)} collective-permute-done((bf16[2,128,1024]{2,1,0:T(8,128)(2,1)S(1)}, bf16[2,128,1024]{2,1,0:T(8,128)(2,1)S(1)}, u32[]{:S(2)}, u32[]{:S(2)}) %collective-permute-start) | collective-permute-done | bytes 524320 | tf_op jit(solution)/shard_map/ppermute | solution.py:41
  24.9 2.8 collective-permute-start.1
  29.3 43.3 %collective-permute-done.1 = bf16[2,128,2048]{2,1,0:T(8,128)(2,1)S(1)} collective-permute-done((bf16[2,128,2048]{2,1,0:T(8,128)(2,1)S(1)}, bf16[2,128,2048]{2,1,0:T(8,128)(2,1)S(1)}, u32[]{:S(2)}, u32[]{:S(2)}) %collective-permute-start.1) | collective-permute-done | bytes 1048608 | tf_op jit(solution)/shard_map/ppermute | solution.py:41
  74.9 9.0 %all-gather = f32[2,1024,8]{1,2,0:T(8,128)S(1)} all-gather(f32[2,128,8]{1,2,0:T(8,128)S(1)} %pad_maximum_fusion.1), channel_id=2, replica_groups=mesh['edata'=4,'expert'=8] {'expert'}, dimensions={1}, use_global_device_ids=true | all-gather | bytes 73728 | tf_op jit(solution)/shard_map/all_gather | solution.py:28
  88.5 77.2 %all-gather.3.cloned.1.call-done = bf16[2,8,128,4096]{3,2,1,0:T(8,128)(2,1)} async-done(((bf16[2,1,128,4096]{3,2,1,0:T(8,128)(2,1)}), bf16[2,8,128,4096]{3,2,1,0:T(8,128)(2,1)}) %all-gather.3.cloned.1.call-update) | async-done | bytes 16777232 | tf_op jit(solution)/shard_map/all_gather | solution.py:47
  165.7 10.2 %fusion.7 = bf16[8,2,80,4096]{3,2,1,0:T(8,128)(2,1)} fusion(bf16[2,8,128,4096]{3,2,1,0:T(8,128)(2,1)} %all-gather.3.cloned.1.call-done, s32[8,128,2,80]{1,3,2,0:T(8,128)S(1)} %convert_reduce_fusion), kind=kOutput, calls=%fused_computation.15 | convolution fusion | flops 1347584000 | bytes 19529728 | tf_op jit(solution)/shard_map/stxc,std->sxcd/dot_general | solution.py:49
  175.9 9.3 %fusion.38 = f32[8,2,80,256]{3,2,0,1:T(8,128)} fusion(bf16[2,256,4096]{2,1,0:T(8,128)(2,1)} %param.11, bf16[8,2,80,4096]{3,2,1,0:T(8,128)(2,1)} %fusion.7), kind=kOutput, calls=%fused_computation.40 | convolution fusion | flops 2684354560 | bytes 15990784 | tf_op jit(solution)/shard_map/sxcd,xfd->sxcf/dot_general | solution.py:54
  185.2 6.3 %fusion.33 = f32[8,2,80,256]{3,2,0,1:T(8,128)} fusion(bf16[2,256,4096]{2,1,0:T(8,128)(2,1)} %param.12, bf16[8,2,80,4096]{3,2,1,0:T(8,128)(2,1)S(1)} %copy-done), kind=kOutput, calls=%fused_computation.39 | convolution fusion | flops 2684354560 | bytes 15990784 | tf_op jit(solution)/shard_map/sxcd,xfd->sxcf/dot_general | solution.py:55
  191.6 8.8 %multiply_convert_fusion = bf16[8,2,80,4096]{3,2,1,0:T(8,128)(2,1)} fusion(f32[8,2,80]{2,1,0:T(2,128)S(1)} %select_reduce_fusion, bf16[2,8,128,4096]{3,2,1,0:T(8,128)(2,1)} %all-gather.3.cloned.1.call-done, s32[8,128,2,80]{1,3,2,0:T(8,128)S(1)} %convert_reduce_fusion), kind=kOutput, calls=%fused_computation.1 | convolution fusion | flops 1352826880 | bytes 19534848 | tf_op jit(solution)/shard_map/stxc,std->sxcd/dot_general | solution.py:52
  200.3 9.4 %multiply_convert_fusion.2 = (bf16[8,2,80,256]{3,2,0,1:T(8,128)(2,1)S(1)}, bf16[8,2,80,256]{3,2,0,1:T(8,128)(2,1)S(1)}) fusion(f32[8,2,80,256]{3,2,0,1:T(8,128)} %fusion.38, f32[8,2,80,256]{3,2,0,1:T(8,128)} %fusion.33, bf16[2,256,4096]{2,1,0:T(8,128)(2,1)} %param.13, bf16[8,2,80,4096]{3,2,1,0:T(8,128)(2,1)} %multiply_convert_fusion), kind=kOutput, calls=%fused_computation.43 | convolution fusion | flops 2688614400 | bytes 18612224 | tf_op jit(solution)/shard_map/sxcd,xfd->sxcf/dot_general | solution.py:59
  209.7 8.5 %fusion.23 = f32[2,8,80,4096]{3,2,1,0:T(8,128)} fusion(bf16[8,2,80,256]{3,2,0,1:T(8,128)(2,1)S(1)} %get-tuple-element.5, bf16[2,256,4096]{2,1,0:T(8,128)(2,1)S(1)} %copy-done.1), kind=kOutput, calls=%fused_computation.28 | convolution fusion | flops 2684354560 | bytes 25821184 | tf_op jit(solution)/shard_map/sxcf,xfd->sxcd/dot_general | solution.py:71
  218.2 13.0 %fusion = bf16[8,2,80,4096]{3,2,0,1:T(8,128)(2,1)} fusion(f32[2,8,80,4096]{3,2,1,0:T(8,128)} %fusion.23, bf16[8,2,80,256]{3,2,0,1:T(8,128)(2,1)S(1)} %get-tuple-element.4, bf16[2,256,4096]{2,1,0:T(8,128)(2,1)} %param.12), kind=kOutput, calls=%fused_computation.2 | convolution fusion | flops 2694840320 | bytes 36306944 | tf_op jit(solution)/shard_map/sxcf,xfd->sxcd/dot_general | solution.py:74
  231.2 9.4 %copy.42 = bf16[8,2,80,4096]{3,2,1,0:T(8,128)(2,1)} copy(bf16[8,2,80,4096]{3,2,0,1:T(8,128)(2,1)} %fusion) | data formatting | bytes 20971520 | tf_op jit(solution)/shard_map/convert_element_type | solution.py:77
  240.6 5.2 %all-to-all-start = ((bf16[8,160,4096]{2,1,0:T(8,128)(2,1)}), bf16[8,160,4096]{2,1,0:T(8,128)(2,1)}, u32[]{:S(2)}, u32[]{:S(2)}) async-start(bf16[8,160,4096]{2,1,0:T(8,128)(2,1)} %bitcast.90), calls=%async_computation | async-start | bytes 20971520 | tf_op jit(solution)/shard_map/all_to_all | solution.py:78
  247.3 7.9 %and_convert_fusion = s32[1024,16,80]{2,1,0:T(8,128)} fusion(pred[1024,80]{1,0:T(8,128)(4,1)S(1)} %iota_compare_fusion.9, pred[1024,16]{1,0:T(8,128)(4,1)S(1)} %copy.35), kind=kLoop, calls=%fused_computation.14 | loop fusion | flops 2621440 | bytes 5341184 | tf_op jit(solution)/shard_map/convert_element_type | solution.py:90
  255.1 9.1 %reshape.193 = s32[128,8,1280]{2,1,0:T(8,128)} reshape(s32[1024,16,80]{2,1,0:T(8,128)} %and_convert_fusion) | data formatting | bytes 10485760 | tf_op jit(solution)/shard_map/convert_element_type | solution.py:90
  264.2 3.7 reduce_sum.37
  268.0 94.4 %all-to-all-done = bf16[8,160,4096]{2,1,0:T(8,128)(2,1)} async-done(((bf16[8,160,4096]{2,1,0:T(8,128)(2,1)}), bf16[8,160,4096]{2,1,0:T(8,128)(2,1)}, u32[]{:S(2)}, u32[]{:S(2)}) %all-to-all-start) | async-done | bytes 10485792 | tf_op jit(solution)/shard_map/all_to_all | solution.py:78
  362.3 6.9 %fusion.58 = f32[128,4096]{1,0:T(8,128)} fusion(bf16[1280,4096]{1,0:T(8,128)(2,1)} %bitcast.28, s32[128,1280]{1,0:T(8,128)S(1)} %reduce_sum.37), kind=kOutput, calls=%fused_computation.55 | convolution fusion | flops 1342341120 | bytes 13238272 | tf_op jit(solution)/shard_map/tq,qd->td/dot_general | solution.py:92
  369.2 9.2 %bitcast_convert_fusion.1 = bf16[2,256,4096]{2,1,0:T(8,128)(2,1)} fusion(bf16[8,2,80,256]{3,2,0,1:T(8,128)(2,1)S(1)} %get-tuple-element.4, bf16[8,2,80,4096]{3,2,1,0:T(8,128)(2,1)} %fusion.7), kind=kOutput, calls=%fused_computation.12 | convolution fusion | flops 2686451712 | bytes 15335424 | tf_op jit(solution)/shard_map/sxcf,sxcd->xfd/dot_general | solution.py:65
  378.4 9.3 %bitcast_convert_fusion.2 = bf16[2,256,4096]{2,1,0:T(8,128)(2,1)} fusion(bf16[8,2,80,256]{3,2,0,1:T(8,128)(2,1)S(1)} %get-tuple-element.5, bf16[8,2,80,4096]{3,2,1,0:T(8,128)(2,1)} %fusion.7), kind=kOutput, calls=%fused_computation.13 | convolution fusion | flops 2686451712 | bytes 15335424 | tf_op jit(solution)/shard_map/sxcf,sxcd->xfd/dot_general | solution.py:62
  387.7 5.3 %bitcast_convert_fusion = bf16[2,256,4096]{2,1,0:T(8,128)(2,1)} fusion(bf16[8,2,80,4096]{3,2,1,0:T(8,128)(2,1)S(1)} %bitcast.92, f32[8,2,80,256]{3,2,0,1:T(8,128)S(1)} %copy-done.5, f32[8,2,80,256]{3,2,0,1:T(8,128)S(1)} %copy-done.4), kind=kOutput, calls=%fused_computation.11 | convolution fusion | flops 2688417792 | bytes 17301504 | tf_op jit(solution)/shard_map/sxcf,sxcd->xfd/dot_general | solution.py:68
  393.1 19.0 %reduce-scatter.2.cloned.1.call-done = f32[128,1024]{1,0:T(8,128)} async-done(((f32[128,4096]{1,0:T(8,128)}), f32[128,1024]{1,0:T(8,128)}) %reduce-scatter.2.cloned.1.call-update) | async-done | bytes 524304 | tf_op jit(solution)/shard_map/reduce_scatter | solution.py:98
  (47 shorter events, 14.3 us)
Async XLA Ops:
  7.2 158.6 %all-gather.3.cloned.1.call-start = ((), (), s32[]{:S(2)}) async-start(), calls=%async_computation.2 | async-start | bytes 18874368 | tf_op jit(solution)/shard_map/all_gather | solution.py:47
  8.3 15.0 %collective-permute-start = (bf16[2,128,1024]{2,1,0:T(8,128)(2,1)S(1)}, bf16[2,128,1024]{2,1,0:T(8,128)(2,1)S(1)}, u32[]{:S(2)}, u32[]{:S(2)}) collective-permute-start(bf16[2,128,1024]{2,1,0:T(8,128)(2,1)S(1)} %pad_maximum_fusion), channel_id=1, source_target_pairs={{0,8},{8,0},{16,24},{24,16},{1,9},{9,1},{17,25},{25,17},{2,10},{10... | collective-permute-start | bytes 1572872 | tf_op jit(solution)/shard_map/ppermute | solution.py:41
  24.9 47.8 %collective-permute-start.1 = (bf16[2,128,2048]{2,1,0:T(8,128)(2,1)S(1)}, bf16[2,128,2048]{2,1,0:T(8,128)(2,1)S(1)}, u32[]{:S(2)}, u32[]{:S(2)}) collective-permute-start(bf16[2,128,2048]{2,1,0:T(8,128)(2,1)S(1)} %maximum_select_fusion.1), channel_id=1, source_target_pairs={{0,16},{8,24},{16,0},{24,8},{1,17},{9,25},{17,1},{25,9},{2,18},{10... | collective-permute-start | bytes 3145736 | tf_op jit(solution)/shard_map/ppermute | solution.py:41
  27.7 47.1 %copy-start.2 = (s32[128,8]{0,1:T(8,128)S(1)}, s32[128,8]{0,1:T(8,128)}, u32[]{:S(2)}) copy-start(s32[128,8]{0,1:T(8,128)} %param.9) | copy-start | bytes 12292
  27.7 47.1 %copy-start.3 = (f32[128,8]{0,1:T(8,128)S(1)}, f32[128,8]{0,1:T(8,128)}, u32[]{:S(2)}) copy-start(f32[128,8]{0,1:T(8,128)} %param.10) | copy-start | bytes 12292
  175.9 9.3 %copy-start = (bf16[8,2,80,4096]{3,2,1,0:T(8,128)(2,1)S(1)}, bf16[8,2,80,4096]{3,2,1,0:T(8,128)(2,1)}, u32[]{:S(2)}) copy-start(bf16[8,2,80,4096]{3,2,1,0:T(8,128)(2,1)} %fusion.7) | copy-start | bytes 31457284
  200.3 9.4 %copy-start.1 = (bf16[2,256,4096]{2,1,0:T(8,128)(2,1)S(1)}, bf16[2,256,4096]{2,1,0:T(8,128)(2,1)}, u32[]{:S(2)}) copy-start(bf16[2,256,4096]{2,1,0:T(8,128)(2,1)} %param.11) | copy-start | bytes 12582916
  240.6 121.7 %all-to-all-start = ((bf16[8,160,4096]{2,1,0:T(8,128)(2,1)}), bf16[8,160,4096]{2,1,0:T(8,128)(2,1)}, u32[]{:S(2)}, u32[]{:S(2)}) async-start(bf16[8,160,4096]{2,1,0:T(8,128)(2,1)} %bitcast.90), calls=%async_computation | async-start | bytes 20971520 | tf_op jit(solution)/shard_map/all_to_all | solution.py:78
  245.8 166.3 %reduce-scatter.2.cloned.1.call-start = ((), (), s32[]{:S(2)}) async-start(), calls=%async_computation.3 | async-start | bytes 2621440 | tf_op jit(solution)/shard_map/reduce_scatter | solution.py:98
  369.2 18.5 %slice-start = ((s8[10485760]{0:T(1024)(128)(4,1)}), s8[4194304]{0:T(1024)(128)(4,1)S(1)}, s32[]{:S(2)}) async-start(s8[10485760]{0:T(1024)(128)(4,1)} %bitcast.91), calls=%async_computation.4 | async-start | bytes 8388608
  369.2 18.5 %slice-start.1 = ((s8[10485760]{0:T(1024)(128)(4,1)}), s8[4194304]{0:T(1024)(128)(4,1)S(1)}, s32[]{:S(2)}) async-start(s8[10485760]{0:T(1024)(128)(4,1)} %bitcast.91), calls=%async_computation.5 | async-start | bytes 8388608
  378.4 9.3 %slice-start.2 = ((s8[10485760]{0:T(1024)(128)(4,1)}), s8[2097152]{0:T(1024)(128)(4,1)S(1)}, s32[]{:S(2)}) async-start(s8[10485760]{0:T(1024)(128)(4,1)} %bitcast.91), calls=%async_computation.6 | async-start | bytes 4194304
  378.4 9.3 %copy-start.4 = (f32[8,2,80,256]{3,2,0,1:T(8,128)S(1)}, f32[8,2,80,256]{3,2,0,1:T(8,128)}, u32[]{:S(2)}) copy-start(f32[8,2,80,256]{3,2,0,1:T(8,128)} %fusion.38) | copy-start | bytes 3932164
  378.4 9.3 %copy-start.5 = (f32[8,2,80,256]{3,2,0,1:T(8,128)S(1)}, f32[8,2,80,256]{3,2,0,1:T(8,128)}, u32[]{:S(2)}) copy-start(f32[8,2,80,256]{3,2,0,1:T(8,128)} %fusion.33) | copy-start | bytes 3932164
Sparse Core Ops, SparseCore 0:
  74.9 90.7 all-gather.2
  369.3 42.7 reduce-scatter.1
